TPU v7x, 32 devices: a whole 2x2x4 slice. The times are simulated.
32 devices in a mesh: img: 2 (over core), band: 4 (over z), pw: 4 (over y, x).
Axes of the slice: x: 2, y: 2, z: 4, core: 2. Of those that a mesh axis runs over, the one named last changes fastest.
Arguments:
- coefficients: bfloat16 [2, 1024, 32, 2048], P('img', None, ('band', 'pw')), may hold values from -6 to 6
- rotation: bfloat16 [2, 1024, 256], P('img'), may hold values from -0.1875 to 0.1875
- positions: int32 [2, 3, 256], P('img'), may hold values from 0 to 63, as said below
- start_pos: int32 [3, 256], replicated, may hold values from 0 to 63, as said below
- end_pos: int32 [3, 256], replicated, may hold values from 0 to 63, as said below
- species: int32 [256], replicated, may hold values from 0 to 3
- depth: float32 [4], replicated, may hold values from 0.5 to 3
Outputs:
- correction: bfloat16 [2, 256, 32, 2048], P('img', None, ('band', 'pw'))
- ritz_values: float32 [2, 256], P('img')
- band_force: float32 [2, 3, 256], P('img')
- along_force: float32 [2], P('img')
Inputs may be any that keep to these rules, and one draw needn't show every extreme that they name: `positions`: grid index of each atom's centre along each dimension. `start_pos`: grid index of each atom's centre along each dimension. `end_pos`: grid index of each atom's centre along each dimension.
All inputs are finite; a program needn't handle non-finite values.
Results may differ from a plain program's by a relative error of at most 0.012.
The roundings to bfloat16 on the way count: a program that leaves them out, or rounds other values in their place, can miss the bound.
Values may be sent and summed in bfloat16 or wider, within the bound.
A program may use at most 128 MiB of HBM per device.

v0:
```python
import math
import jax
import jax.numpy as jnp
from jax import lax
from jax.sharding import PartitionSpec as P

G = 64
W = 32
BANDS = 1024
BLOCK = 256
SPECIES = 4
kinetic_scale = 0.01
sigma_cells = 3.0
spring_constant = 2.0
epsilon = 1e-06
highest = lax.Precision.HIGHEST


def passed_along(block, axis, distance):
    devices = range(lax.axis_size(axis))
    route = [(i - distance, i) for i in devices if i - distance in devices]
    return lax.ppermute(block, axis, route)


def phases(box_order, box_size, grid_size):
    wavenum = box_order - box_size // 2
    grid_cells = jnp.arange(grid_size, dtype=jnp.int32)
    turn_count = jnp.mod(wavenum[:, None] * grid_cells[None, :], grid_size)
    return turn_count.astype(jnp.float32) * (2.0 * math.pi / grid_size)


def forward_table(box_order, box_size, grid_size):
    angle_tab = phases(box_order, box_size, grid_size)
    cosine = jnp.cos(angle_tab) / math.sqrt(box_size)
    sine_part = jnp.sin(angle_tab) / math.sqrt(box_size)
    dft_table = jnp.stack(
        [jnp.stack([cosine, sine_part], 1), jnp.stack([-sine_part, cosine], 1)], 0
    )
    return dft_table.astype(jnp.bfloat16)


def inverse_table(box_order, box_size, grid_size):
    angle_tab = phases(box_order, box_size, grid_size).T
    factor = math.sqrt(box_size) / grid_size
    cosine = jnp.cos(angle_tab) * factor
    sine_part = jnp.sin(angle_tab) * factor
    dft_table = jnp.stack(
        [jnp.stack([cosine, -sine_part], 1), jnp.stack([sine_part, cosine], 1)], 0
    )
    return dft_table.astype(jnp.bfloat16)


def section_zy(coeff_block, table_z, table_y):
    leading = coeff_block.shape[0]
    planes = coeff_block.shape[1]
    split_up = coeff_block.reshape(leading, planes, W, 2, W)
    along_z = jnp.einsum(
        "blyck,ckdn->blydn", split_up, table_z, preferred_element_type=jnp.float32
    ).astype(jnp.bfloat16)
    along_y = jnp.einsum(
        "blycz,cydm->blmdz", along_z, table_y, preferred_element_type=jnp.float32
    ).astype(jnp.bfloat16)
    return along_y.reshape(leading, planes, G * 2 * G)


def section_x(arrived, table_x):
    leading = arrived.shape[0]
    y_rows = arrived.shape[2] // (2 * G)
    split_up = arrived.reshape(leading, W, y_rows, 2, G)
    return jnp.einsum("bxycz,cxdn->bnydz", split_up, table_x, preferred_element_type=jnp.float32)


def section_x_inverse(weighted, table_x):
    leading = weighted.shape[0]
    y_rows = weighted.shape[2]
    along_x = jnp.einsum(
        "bnydz,dncx->bxycz", weighted, table_x, preferred_element_type=jnp.float32
    ).astype(jnp.bfloat16)
    return along_x.reshape(leading, W, y_rows * 2 * G)


def section_zy_inverse(returned, table_y, table_z):
    leading = returned.shape[0]
    planes = returned.shape[1]
    split_up = returned.reshape(leading, planes, G, 2, G)
    along_y = jnp.einsum(
        "blmdz,dmcy->blycz", split_up, table_y, preferred_element_type=jnp.float32
    ).astype(jnp.bfloat16)
    along_z = jnp.einsum("blydn,dnck->blyck", along_y, table_z, preferred_element_type=jnp.float32)
    return along_z.reshape(leading, planes, W * 2 * W)


def wrap_offset(values):
    return jnp.mod(values + G // 2, G) - G // 2


def gaussians(coords, grid_cells):
    offset = wrap_offset(grid_cells[None, :] - coords[:, None]).astype(jnp.float32)
    return (jnp.exp(-offset * offset / (2.0 * sigma_cells * sigma_cells)), offset)


def atom_tables(own_pos, y_cells):
    grid_cells = jnp.arange(G, dtype=jnp.int32)
    gauss_x, offset_x = gaussians(own_pos[0], grid_cells)
    gauss_y, offset_y = gaussians(own_pos[1], y_cells)
    gauss_z, offset_z = gaussians(own_pos[2], grid_cells)
    return (gauss_x, offset_x, gauss_y, offset_y, gauss_z, offset_z)


def local_potential(tables, strength):
    gauss_x, offset_x, gauss_y, offset_y, gauss_z, offset_z = tables
    atom_count = gauss_x.shape[0]
    joined = (gauss_y[:, :, None] * gauss_z[:, None, :]).reshape(atom_count, -1)
    potential = jnp.dot((strength[:, None] * gauss_x).T, joined, precision=highest)
    return (potential, joined)


def atom_forces(density, tables, joined, strength):
    gauss_x, offset_x, gauss_y, offset_y, gauss_z, offset_z = tables
    atom_count = gauss_x.shape[0]
    with_y = ((gauss_y * offset_y)[:, :, None] * gauss_z[:, None, :]).reshape(atom_count, -1)
    with_z = (gauss_y[:, :, None] * (gauss_z * offset_z)[:, None, :]).reshape(atom_count, -1)
    stacked = jnp.concatenate([joined, with_y, with_z], 0)
    moments = jnp.dot(density, stacked.T, precision=highest)
    prefactor = -strength / (sigma_cells * sigma_cells)
    force_x = prefactor * jnp.sum(gauss_x * offset_x * moments[:, :atom_count].T, 1)
    force_y = prefactor * jnp.sum(gauss_x * moments[:, atom_count : 2 * atom_count].T, 1)
    force_z = prefactor * jnp.sum(gauss_x * moments[:, 2 * atom_count :].T, 1)
    return jnp.stack([force_x, force_y, force_z], 0)


def space_work(in_space, own_pos, strength, y_rows):
    y_cells = jnp.arange(y_rows, dtype=jnp.int32)
    tables = atom_tables(own_pos, y_cells)
    potential, joined = local_potential(tables, strength)
    grid_potential = potential.reshape(G, y_rows, G)
    density = jnp.sum(in_space * in_space, axis=(0, 3)).reshape(G, y_rows * G) / BLOCK
    force_part = atom_forces(density, tables, joined, strength)
    weighted = (in_space * grid_potential[:, :, None, :]).astype(jnp.bfloat16)
    return (weighted, force_part)


def kinetic_table(x_cells):
    entries = jnp.arange(W * 2 * W, dtype=jnp.int32)
    wave_y = entries // (2 * W) - W // 2
    wave_z = jnp.mod(entries, W) - W // 2
    wave_x = x_cells - W // 2
    squared = wave_x[:, None] * wave_x[:, None] + (wave_y * wave_y + wave_z * wave_z)[None, :]
    return kinetic_scale * 0.5 * squared.astype(jnp.float32)


def rotate_quarter(values):
    leading = values.shape[0]
    middle = values.shape[1]
    split_up = values.reshape(leading, middle, W, 2, W)
    turned = jnp.stack([-split_up[:, :, :, 1, :], split_up[:, :, :, 0, :]], 3)
    return turned.reshape(values.shape)


def chain_forces(force, own_pos, before, after):
    ahead_step = wrap_offset(after - own_pos).astype(jnp.float32)
    behind = wrap_offset(own_pos - before).astype(jnp.float32)
    tangent_raw = ahead_step + behind
    entries = 3 * own_pos.shape[1]
    tangent = (
        tangent_raw * lax.rsqrt(jnp.mean(tangent_raw * tangent_raw) + epsilon) / math.sqrt(entries)
    )
    length_ahead = jnp.sqrt(entries * (jnp.mean(ahead_step * ahead_step) + epsilon))
    length_behind = jnp.sqrt(entries * (jnp.mean(behind * behind) + epsilon))
    along_path = jnp.sum(force * tangent)
    band_push = (
        force - along_path * tangent + spring_constant * (length_ahead - length_behind) * tangent
    )
    return (band_push, along_path)


def body(coefficients, rotation, positions, start_pos, end_pos, species, depth):
    coeff_all = coefficients[0]
    planes = coeff_all.shape[1]
    flat_all = coeff_all.reshape(BANDS, -1)
    orbitals = jnp.einsum("ib,ik->bk", rotation[0], flat_all, preferred_element_type=jnp.float32)
    orbitals = orbitals.astype(jnp.bfloat16).reshape(BLOCK, planes, W * 2 * W)
    kind_ids = jnp.arange(SPECIES, dtype=jnp.int32)
    strength = jnp.sum(jnp.where(species[:, None] == kind_ids[None, :], depth[None, :], 0.0), 1)
    own_pos = positions[0]
    natural = jnp.arange(W, dtype=jnp.int32)
    table_f = forward_table(natural, W, G)
    table_i = inverse_table(natural, W, G)
    whole_vectors = lax.all_to_all(
        orbitals, ("band", "pw"), split_axis=0, concat_axis=1, tiled=True
    )
    spread = section_zy(whole_vectors, table_f, table_f)
    weighted, force_part = space_work(section_x(spread, table_f), own_pos, strength, G)
    partial_apply = section_zy_inverse(section_x_inverse(weighted, table_i), table_i, table_i)
    applied = lax.all_to_all(partial_apply, ("band", "pw"), split_axis=1, concat_axis=0, tiled=True)
    x_cells = lax.axis_index(("band", "pw")) * planes + jnp.arange(planes, dtype=jnp.int32)
    kinetic = kinetic_table(x_cells)
    orbitals_wide = orbitals.astype(jnp.float32)
    hamiltonian = kinetic[None] * orbitals_wide + applied
    numerator = jnp.sum(orbitals_wide * hamiltonian, axis=(1, 2))
    denominator = jnp.sum(orbitals_wide * orbitals_wide, axis=(1, 2))
    numerator, denominator, atom_force = lax.psum(
        (numerator, denominator, force_part), ("band", "pw")
    )
    npw_total = W * W * W
    ritz_values = numerator / npw_total / (denominator / npw_total + epsilon)
    residual = hamiltonian - ritz_values[:, None, None] * orbitals_wide
    search = (residual / (1.0 + kinetic)[None]).astype(jnp.bfloat16)
    search_pair = jnp.concatenate(
        [search.reshape(BLOCK, -1), (-rotate_quarter(search)).reshape(BLOCK, -1)], 0
    )
    intersections = (
        jnp.einsum("ik,jk->ij", flat_all, search_pair, preferred_element_type=jnp.float32)
        / npw_total
    )
    intersections = lax.psum(intersections, ("band", "pw")).astype(jnp.bfloat16)
    projected = jnp.einsum("ij,ik->jk", intersections, flat_all, preferred_element_type=jnp.float32)
    projection = projected[:BLOCK].reshape(BLOCK, planes, -1) + rotate_quarter(
        projected[BLOCK:].reshape(BLOCK, planes, -1)
    )
    correction = (search.astype(jnp.float32) - projection).astype(jnp.bfloat16)
    image_idx = lax.axis_index("img")
    before = passed_along(own_pos, "img", 1)
    after = passed_along(own_pos, "img", -1)
    before = jnp.where(image_idx == 0, start_pos, before)
    after = jnp.where(image_idx == lax.axis_size("img") - 1, end_pos, after)
    band_push, along_path = chain_forces(atom_force, own_pos, before, after)
    return (correction[None], ritz_values[None], band_push[None], along_path[None])


def solution(mesh):
    in_specs = (
        P("img", None, ("band", "pw"), None),
        P("img", None, None),
        P("img", None, None),
        P(),
        P(),
        P(),
        P(),
    )
    out_specs = (
        P("img", None, ("band", "pw"), None),
        P("img", None),
        P("img", None, None),
        P("img"),
    )
    return jax.shard_map(body, mesh=mesh, in_specs=in_specs, out_specs=out_specs, check_vma=False)
```

profile of v0, /device:TPU:0, one launch (start us, length us, event | category | flops | bytes accessed | tf_op | source)
XLA Modules:
  0.0 592.1 jit_solution(8768601264481166253)
XLA Ops:
  0.6 0.0 copy-start
  0.6 12.1 %copy.141 = bf16[128,8,2,2048]{3,1,2,0:T(8,128)(2,1)} copy(bf16[128,8,2,2048]{3,2,1,0:T(2,128)(2,1)} %bitcast.208) | data formatting | bytes 16777216
  12.7 5.8 convolution_convert_fusion
  18.5 2.8 reshape.676
  21.3 8.6 %all-to-all-start = ((bf16[256,2,2048]{2,1,0:T(2,128)(2,1)}), bf16[256,2,2048]{2,1,0:T(2,128)(2,1)}, u32[]{:S(2)}, u32[]{:S(2)}) async-start(bf16[256,2,2048]{2,1,0:T(2,128)(2,1)} %reshape.676), calls=%async_computation | async-start | bytes 4194304 | tf_op jit(solution)/shard_map/all_to_all | solution.py:189
  29.9 0.2 fusion.111
  30.1 0.2 negate_convert_fusion.1
  30.3 0.1 select_reduce_fusion
  30.4 0.1 fusion.79
  30.5 7.5 %fusion.29 = f32[64,64,64]{2,0,1:T(8,128)} fusion(f32[256,64]{0,1:T(8,128)S(1)} %get-tuple-element.67, f32[256,64]{0,1:T(8,128)S(1)} %get-tuple-element.74, s32[256]{0:T(256)S(1)} %bitcast.217, f32[256]{0:T(256)S(1)} %select_reduce_fusion), kind=kOutput, calls=%fused_computation.35 | convolution fusion | flops 806666240 | bytes 1181696 | tf_op jit(solution)/shard_map/dot_general | solution.py:114
  37.9 35.0 %all-to-all-done = bf16[256,2,2048]{2,1,0:T(2,128)(2,1)} async-done(((bf16[256,2,2048]{2,1,0:T(2,128)(2,1)}), bf16[256,2,2048]{2,1,0:T(2,128)(2,1)}, u32[]{:S(2)}, u32[]{:S(2)}) %all-to-all-start) | async-done | bytes 2097184 | tf_op jit(solution)/shard_map/all_to_all | solution.py:189
  72.9 2.5 copy.101
  75.4 1.5 copy.102
  76.9 17.9 %reshape.677 = bf16[16,32,32,2,32]{4,3,2,0,1:T(2,128)(2,1)} reshape(bf16[16,16,2,2048]{3,0,2,1:T(8,128)(2,1)} %copy.102) | data formatting | bytes 4194304 | tf_op jit(solution)/shard_map/reshape | solution.py:56
  94.8 12.6 %fusion.20 = bf16[16,32,64,2,64]{4,2,1,0,3:T(8,128)(2,1)} fusion(bf16[16,32,32,2,32,1]{4,3,2,0,1,5:T(2,128)(2,1)} %bitcast.203, bf16[1,32,2,64]{3,1,0,2:T(8,128)(2,1)S(1)} %get-tuple-element.57, bf16[1,32,2,64]{3,1,0,2:T(8,128)(2,1)S(1)} %get-tuple-element.56), kind=kOutput, calls=%fused_computation.24 | convolution fusion | flops 811663360 | bytes 10502144 | tf_op jit(solution)/shard_map/blycz,cydm->blmdz/dot_general | solution.py:60
  107.4 28.7 %fusion.1 = (f32[64,64,64]{2,0,1:T(8,128)}, bf16[16,64,64,2,64]{4,1,2,0,3:T(8,128)(2,1)}) fusion(f32[64,64,64]{2,0,1:T(8,128)} %fusion.29, bf16[16,32,64,2,64]{4,2,1,0,3:T(8,128)(2,1)} %fusion.20, bf16[1,32,2,64]{3,1,0,2:T(8,128)(2,1)S(1)} %get-tuple-element.57, bf16[1,32,2,64]{3,1,0,2:T(8,128)(2,1)S(1)} %get-tuple-element.56), kind=kOutput, calls=%fused_computation.3 | convolution fusion | flops 1107066880 | bytes 27279360 | tf_op jit(solution)/shard_map/bxycz,cxdn->bnydz/dot_general | solution.py:70
  136.1 18.9 %fusion.6 = bf16[16,32,64,2,64,1]{4,1,2,0,3,5:T(8,128)(2,1)} fusion(bf16[16,64,64,2,64]{4,1,2,0,3:T(8,128)(2,1)} %get-tuple-element.40, bf16[1,64,2,32]{1,3,0,2:T(8,128)(2,1)S(1)} %get-tuple-element.55, bf16[1,64,2,32]{1,3,0,2:T(8,128)(2,1)S(1)} %get-tuple-element.54), kind=kOutput, calls=%fused_computation.10 | convolution fusion | flops 1077968896 | bytes 25182208 | tf_op jit(solution)/shard_map/bnydz,dncx->bxycz/dot_general | solution.py:76
  155.0 19.3 %convolution_bitcast_fusion = f32[16,32,32,2,32]{4,2,3,1,0:T(8,128)} fusion(bf16[16,32,64,2,64,1]{4,1,2,0,3,5:T(8,128)(2,1)} %fusion.6, bf16[1,64,2,32]{1,3,0,2:T(8,128)(2,1)S(1)} %get-tuple-element.55, bf16[1,64,2,32]{1,3,0,2:T(8,128)(2,1)S(1)} %get-tuple-element.54), kind=kOutput, calls=%fused_computation.25 | convolution fusion | flops 807469056 | bytes 12599296 | tf_op jit(solution)/shard_map/blydn,dnck->blyck/dot_general | solution.py:89
  174.3 28.6 %copy.138 = f32[16,32,32,2,32]{4,3,2,0,1:T(2,128)} copy(f32[16,32,32,2,32]{4,2,3,1,0:T(8,128)} %convolution_bitcast_fusion) | data formatting | bytes 8388608 | tf_op jit(solution)/shard_map/reshape | solution.py:90
  202.9 21.7 %reshape.699 = f32[16,32,2048]{2,0,1:T(8,128)} reshape(f32[16,32,32,2,32]{4,3,2,0,1:T(2,128)} %copy.138) | data formatting | bytes 8388608 | tf_op jit(solution)/shard_map/reshape | solution.py:90
  224.6 10.1 %all-to-all-start.1 = ((f32[16,32,2048]{2,0,1:T(8,128)}), f32[16,32,2048]{2,0,1:T(8,128)}, u32[]{:S(2)}, u32[]{:S(2)}) async-start(f32[16,32,2048]{2,0,1:T(8,128)} %reshape.699), calls=%async_computation.1 | async-start | bytes 8388608 | tf_op jit(solution)/shard_map/all_to_all | solution.py:195
  234.7 1.3 collective-permute-start
  236.0 3.0 collective-permute-start.1
  239.1 0.1 fusion.83
  239.2 0.1 convert_multiply_fusion.4
  239.3 0.1 convert_multiply_fusion.6
  239.4 5.0 broadcast_multiply_fusion.2
  244.4 0.1 add.348
  244.5 3.0 copy.112
  247.5 5.1 reshape.682
  252.7 0.6 multiply_reduce_fusion.3
  254.0 0.6 multiply_reduce_fusion
  256.0 1.8 broadcast_multiply_fusion.4
  257.8 2.5 copy.119
  260.3 3.1 div.129
  263.4 12.6 %fusion.14 = f32[64,768]{1,0:T(8,128)S(1)} fusion(f32[64,4096]{1,0:T(8,128)} %div.129, f32[256,4096]{0,1:T(8,128)} %bitcast.212, f32[256,4096]{0,1:T(8,128)} %bitcast.213, f32[256,4096]{0,1:T(8,128)} %bitcast.211), kind=kOutput, calls=%fused_computation.18 | convolution fusion | flops 2422210560 | bytes 13828096 | tf_op jit(solution)/shard_map/dot_general | solution.py:124
  276.1 0.1 fusion.75
  276.2 36.9 %all-to-all-done.1 = f32[16,32,2048]{2,0,1:T(8,128)} async-done(((f32[16,32,2048]{2,0,1:T(8,128)}), f32[16,32,2048]{2,0,1:T(8,128)}, u32[]{:S(2)}, u32[]{:S(2)}) %all-to-all-start.1) | async-done | bytes 4194336 | tf_op jit(solution)/shard_map/all_to_all | solution.py:195
  313.0 5.5 copy.110
  318.5 4.7 copy.109
  323.2 5.9 %copy.143 = f32[32,8,2,2048]{3,1,2,0:T(8,128)} copy(f32[32,8,2,2048]{3,2,1,0:T(2,128)S(1)} %bitcast.206) | data formatting | bytes 8388608
  329.1 18.0 %all_to_all.36 = f32[256,2,32,2,32]{4,3,2,0,1:T(2,128)} reshape(f32[16,16,2,2048]{3,1,0,2:T(8,128)} %copy.109) | data formatting | bytes 8388608 | tf_op jit(solution)/shard_map/all_to_all | solution.py:195
  347.1 20.8 %copy.114 = f32[256,2,32,2,32]{0,4,3,2,1:T(8,128)} copy(f32[256,2,32,2,32]{4,3,2,0,1:T(2,128)} %all_to_all.36) | data formatting | bytes 8388608 | tf_op jit(solution)/shard_map/all_to_all | solution.py:195
  367.9 3.3 fusion.37
  371.1 54.3 %all-reduce.1 = (f32[256]{0:T(256)S(1)}, f32[256]{0:T(256)S(1)}) all-reduce(f32[256]{0:T(256)S(1)} %get-tuple-element.25, f32[256]{0:T(256)S(1)} %get-tuple-element.24), channel_id=1, replica_groups=mesh['img'=2,'band'=4,'pw'=4] {'band','pw'}, use_global_device_ids=true, to_apply=%region_4.5 | all-reduce | flops 512 | bytes 4096 | tf_op jit(solution)/shard_map/psum | solution.py:202
  425.5 4.6 fusion.41
  430.2 0.8 copy-done.3
  431.0 1.5 divide_convert_fusion
  432.5 0.1 slice_negate_fusion.1
  432.6 0.2 maximum_negate_fusion
  432.8 2.9 copy.115
  435.7 8.2 %multiply_bitcast_fusion = f32[1024,512]{0,1:T(8,128)S(1)} fusion(bf16[1024,4096]{1,0:T(8,128)(2,1)} %bitcast.199, bf16[256,4096]{1,0:T(8,128)(2,1)} %copy.115, bf16[256,4096]{1,0:T(8,128)(2,1)} %fusion.41), kind=kOutput, calls=%fused_computation.59 | convolution fusion | flops 4303880192 | bytes 14680064 | tf_op jit(solution)/shard_map/ik,jk->ij/dot_general | solution.py:213
  444.0 97.9 %all-reduce.3 = (bf16[1024,512]{0,1:T(8,128)(2,1)}, f32[3,256]{1,0:T(4,128)S(1)}) all-reduce(f32[1024,512]{0,1:T(8,128)S(1)} %multiply_bitcast_fusion, f32[3,256]{1,0:T(4,128)S(1)} %pad_maximum_fusion.9), channel_id=1, replica_groups=mesh['img'=2,'band'=4,'pw'=4] {'band','pw'}, use_global_device_ids=true, to_apply=%region_5.6 | all-reduce | flops 525056 | bytes 3151872 | tf_op jit(solution)/shard_map/psum | solution.py:216
  541.8 0.6 multiply_reduce_fusion.2
  543.1 0.6 broadcast_in_dim.21
  543.7 7.2 %fusion.152 = f32[512,4096]{1,0:T(8,128)S(1)} fusion(bf16[1024,512]{0,1:T(8,128)(2,1)} %get-tuple-element.29, bf16[1024,4096]{1,0:T(8,128)(2,1)} %bitcast.200), kind=kOutput, calls=%fused_computation.217 | convolution fusion | flops 4294967296 | bytes 17825792 | tf_op jit(solution)/shard_map/ij,ik->jk/dot_general | solution.py:217
  550.9 3.8 fusion.146
  554.6 5.6 copy.116
  560.2 2.8 slice_negate_fusion
  563.0 2.4 pad_maximum_fusion
  565.5 5.4 copy.118
  570.9 6.6 %reshape.680 = f32[1,256,2,2048]{3,2,1,0:T(2,128)} reshape(f32[256,4096]{1,0:T(8,128)} %get-tuple-element.41) | data formatting | bytes 8388608 | tf_op jit(solution)/shard_map/reshape | solution.py:218
  577.4 10.7 %fusion.35 = bf16[1,256,2,2048]{3,1,2,0:T(8,128)(2,1)S(1)} fusion(f32[1,256,2,2048]{3,1,2,0:T(8,128)} %copy.118, f32[1,256,2,2048]{3,2,1,0:T(2,128)} %reshape.680, f32[16,16,2,2048]{3,1,0,2:T(8,128)} %copy.109, f32[1,256,2,2048]{3,2,1,0:T(2,128)} %reshape.682, f32[2,2048]{1,0:T(2,128)S(1)} %get-tuple-element.53, f32[256]{0:T(256)S(1)} %add_divide_fusion, ...), kind=kLoop, calls=%fused_computation.43 | loop fusion | flops 10485760 | bytes 18908160 | tf_op jit(solution)/shard_map/convert_element_type | solution.py:221
  588.1 3.5 copy.120
  (34 shorter events, 0.1 us)
Async XLA Ops:
  0.6 12.1 %copy-start = (bf16[1,1024,256]{2,1,0:T(8,128)(2,1)S(1)}, bf16[1,1024,256]{2,1,0:T(8,128)(2,1)}, u32[]{:S(2)}) copy-start(bf16[1,1024,256]{2,1,0:T(8,128)(2,1)} %param.8) | copy-start | bytes 1572868
  18.5 11.8 %copy-start.8 = (s32[256]{0:T(256)S(1)}, s32[256]{0:T(256)}, u32[]{:S(2)}) copy-start(s32[256]{0:T(256)} %param.12) | copy-start | bytes 3076
  18.5 11.8 %copy-start.9 = (f32[4]{0:T(128)S(1)}, f32[4]{0:T(128)}, u32[]{:S(2)}) copy-start(f32[4]{0:T(128)} %param.13) | copy-start | bytes 52
  18.5 11.9 %copy-start.4 = (s32[1,3,256]{2,0,1:T(1,128)S(1)}, s32[1,3,256]{2,0,1:T(1,128)}, u32[]{:S(2)}) copy-start(s32[1,3,256]{2,0,1:T(1,128)} %param.9) | copy-start | bytes 9220
  21.3 51.6 %all-to-all-start = ((bf16[256,2,2048]{2,1,0:T(2,128)(2,1)}), bf16[256,2,2048]{2,1,0:T(2,128)(2,1)}, u32[]{:S(2)}, u32[]{:S(2)}) async-start(bf16[256,2,2048]{2,1,0:T(2,128)(2,1)} %reshape.676), calls=%async_computation | async-start | bytes 4194304 | tf_op jit(solution)/shard_map/all_to_all | solution.py:189
  224.6 88.5 %all-to-all-start.1 = ((f32[16,32,2048]{2,0,1:T(8,128)}), f32[16,32,2048]{2,0,1:T(8,128)}, u32[]{:S(2)}, u32[]{:S(2)}) async-start(f32[16,32,2048]{2,0,1:T(8,128)} %reshape.699), calls=%async_computation.1 | async-start | bytes 8388608 | tf_op jit(solution)/shard_map/all_to_all | solution.py:195
  234.7 18.0 %collective-permute-start = (s32[3,256]{1,0:T(4,128)S(1)}, s32[3,256]{1,0:T(4,128)S(1)}, u32[]{:S(2)}, u32[]{:S(2)}) collective-permute-start(s32[3,256]{1,0:T(4,128)S(1)} %bitcast.224), channel_id=1, source_target_pairs={{16,0},{17,1},{18,2},{19,3},{20,4},{21,5},{22,6},{23,7},{24,8},{25... | collective-permute-start | bytes 9224 | tf_op jit(solution)/shard_map/ppermute | solution.py:22
  236.0 16.7 %collective-permute-start.1 = (s32[3,256]{1,0:T(4,128)S(1)}, s32[3,256]{1,0:T(4,128)S(1)}, u32[]{:S(2)}, u32[]{:S(2)}) collective-permute-start(s32[3,256]{1,0:T(4,128)S(1)} %bitcast.225), channel_id=1, source_target_pairs={{0,16},{1,17},{2,18},{3,19},{4,20},{5,21},{6,22},{7,23},{8,24},{9,... | collective-permute-start | bytes 9224 | tf_op jit(solution)/shard_map/ppermute | solution.py:22
  247.5 5.2 copy-start.6
  247.5 5.2 copy-start.7
  425.5 151.9 %copy-start.5 = (f32[256]{0:T(256)}, f32[256]{0:T(256)S(1)}, u32[]{:S(2)}) copy-start(f32[256]{0:T(256)S(1)} %add_divide_fusion) | copy-start | bytes 3076
  425.5 4.7 copy-start.2
  425.5 5.5 copy-start.3
  577.4 14.2 %copy-start.1 = (bf16[1,1024,256]{2,1,0:T(8,128)(2,1)S(1)}, bf16[1,1024,256]{2,1,0:T(8,128)(2,1)}, u32[]{:S(2)}) copy-start(bf16[1,1024,256]{2,1,0:T(8,128)(2,1)} %param.8) | copy-start | bytes 1572868
where the time goes:
time: 600 us; the launch traced here: 592 us
  local copies, waits for them, and re-layouts  185 us (31%)
  blocking collectives  152 us (25%)
  matrix products  121 us (20%)
  waiting for transfers between devices  71.8 us (12%)
  other arithmetic  35.2 us (6%)
  starting transfers between devices  23 us (4%)
    psum x1, blocking collectives, body(): intersections = lax.psum(intersections, ('band', 'pw')).astype(jnp.bfloat16)  97.9 us
    psum x1, blocking collectives, body(): lax.psum((numerator, denominator, force_part), ('band', 'pw'))  54.3 us
    reshape x2, local copies, waits for them, and re-layouts, section_zy_inverse(): return along_z.reshape(leading, planes, W * 2 * W)  50.3 us
    all_to_all x4, local copies, waits for them, and re-layouts, body(): lax.all_to_all(partial_apply, ('band', 'pw'), split_axis=1, concat_axis=0...  48.9 us
    all_to_all x1, waiting for transfers between devices, body(): lax.all_to_all(partial_apply, ('band', 'pw'), split_axis=1, concat_axis=0...  36.9 us
    all_to_all x1, waiting for transfers between devices, body(): lax.all_to_all(orbitals, ('band', 'pw'), split_axis=0, concat_axis=1, til...  35 us
    dot_general x1, matrix products, section_x(): jnp.einsum('bxycz,cxdn->bnydz', split_up, table_x, preferred_element_type...  28.7 us
    unnamed x26, local copies, waits for them, and re-layouts  22.4 us
  transfers between devices with their start and end apart: 4, of which 2 were waited for; matrix products, arithmetic and copies ran while one was open for 7% of the time, Pallas kernels for 0%

commit v1 on v0

--- a/solution.py
+++ b/solution.py
@@ -14,6 +14,11 @@
 spring_constant = 2.0
 epsilon = 1e-06
 highest = lax.Precision.HIGHEST
+
+
+def by_each_axis(x, one, other):
+    inner = lax.psum(x, one)
+    return lax.psum(inner, other)
 
 
 def passed_along(block, axis, distance):
@@ -199,8 +204,8 @@
     hamiltonian = kinetic[None] * orbitals_wide + applied
     numerator = jnp.sum(orbitals_wide * hamiltonian, axis=(1, 2))
     denominator = jnp.sum(orbitals_wide * orbitals_wide, axis=(1, 2))
-    numerator, denominator, atom_force = lax.psum(
-        (numerator, denominator, force_part), ("band", "pw")
+    numerator, denominator, atom_force = by_each_axis(
+        (numerator, denominator, force_part), "pw", "band"
     )
     npw_total = W * W * W
     ritz_values = numerator / npw_total / (denominator / npw_total + epsilon)

time: 600 us -> 577 us (0.962)
  blocking collectives: 152 us -> 132 us
    psum x1 -> x2, blocking collectives: 54.3 us -> 34.6 us  [the longest x1 19.3 us: by_each_axis(): return lax.psum(inner, other)]
    unnamed x26 -> x28, local copies, waits for them, and re-layouts: 22.4 us -> 22.4 us
  transfers between devices with their start and end apart: 4 -> 4, of which waited for: 2 -> 2; matrix products, arithmetic and copies ran while one was open for 7% -> 8% of each run, Pallas kernels for 0% -> 0%
where the time goes in v1:
time: 577 us; the launch traced here: 570 us
  local copies, waits for them, and re-layouts  185 us (32%)
  blocking collectives  132 us (23%)
  matrix products  121 us (21%)
  waiting for transfers between devices  71.8 us (12%)
  other arithmetic  33.1 us (6%)
  starting transfers between devices  23 us (4%)
    psum x1, blocking collectives, body(): intersections = lax.psum(intersections, ('band', 'pw')).astype(jnp.bfloat16)  97.3 us
    reshape x2, local copies, waits for them, and re-layouts, section_zy_inverse(): return along_z.reshape(leading, planes, W * 2 * W)  50.3 us
    all_to_all x4, local copies, waits for them, and re-layouts, body(): lax.all_to_all(partial_apply, ('band', 'pw'), split_axis=1, concat_axis=0...  48.9 us
    all_to_all x1, waiting for transfers between devices, body(): lax.all_to_all(partial_apply, ('band', 'pw'), split_axis=1, concat_axis=0...  36.9 us
    all_to_all x1, waiting for transfers between devices, body(): lax.all_to_all(orbitals, ('band', 'pw'), split_axis=0, concat_axis=1, til...  35 us
    dot_general x1, matrix products, section_x(): jnp.einsum('bxycz,cxdn->bnydz', split_up, table_x, preferred_element_type...  28.7 us
    unnamed x28, local copies, waits for them, and re-layouts  22.4 us
    psum x1, blocking collectives, by_each_axis(): return lax.psum(inner, other)  19.3 us
  transfers between devices with their start and end apart: 4, of which 2 were waited for; matrix products, arithmetic and copies ran while one was open for 8% of the time, Pallas kernels for 0%

profile of v1, /device:TPU:0, one launch (start us, length us, event | category | flops | bytes accessed | tf_op | source)
XLA Modules:
  0.0 569.7 jit_solution(11406081001757413797)
XLA Ops:
  0.6 12.1 %copy.141 = bf16[128,8,2,2048]{3,1,2,0:T(8,128)(2,1)} copy(bf16[128,8,2,2048]{3,2,1,0:T(2,128)(2,1)} %bitcast.208) | data formatting | bytes 16777216
  12.7 5.8 %convolution_convert_fusion = bf16[256,4096]{1,0:T(8,128)(2,1)S(1)} fusion(bf16[1024,4096]{1,0:T(8,128)(2,1)} %bitcast.198, bf16[1,1024,256]{2,1,0:T(8,128)(2,1)S(1)} %copy-done), kind=kOutput, calls=%fused_computation.29 | convolution fusion | flops 2148532224 | bytes 11010048 | tf_op jit(solution)/shard_map/ib,ik->bk/dot_general | solution.py:186
  18.5 2.8 reshape.676
  21.3 8.6 %all-to-all-start = ((bf16[256,2,2048]{2,1,0:T(2,128)(2,1)}), bf16[256,2,2048]{2,1,0:T(2,128)(2,1)}, u32[]{:S(2)}, u32[]{:S(2)}) async-start(bf16[256,2,2048]{2,1,0:T(2,128)(2,1)} %reshape.676), calls=%async_computation | async-start | bytes 4194304 | tf_op jit(solution)/shard_map/all_to_all | solution.py:194
  29.9 0.2 fusion.111
  30.1 0.2 negate_convert_fusion.1
  30.3 0.1 select_reduce_fusion
  30.4 0.1 fusion.79
  30.5 7.5 %fusion.29 = f32[64,64,64]{2,0,1:T(8,128)} fusion(f32[256,64]{0,1:T(8,128)S(1)} %get-tuple-element.69, f32[256,64]{0,1:T(8,128)S(1)} %get-tuple-element.76, s32[256]{0:T(256)S(1)} %bitcast.217, f32[256]{0:T(256)S(1)} %select_reduce_fusion), kind=kOutput, calls=%fused_computation.35 | convolution fusion | flops 806666240 | bytes 1181696 | tf_op jit(solution)/shard_map/dot_general | solution.py:119
  37.9 35.0 %all-to-all-done = bf16[256,2,2048]{2,1,0:T(2,128)(2,1)} async-done(((bf16[256,2,2048]{2,1,0:T(2,128)(2,1)}), bf16[256,2,2048]{2,1,0:T(2,128)(2,1)}, u32[]{:S(2)}, u32[]{:S(2)}) %all-to-all-start) | async-done | bytes 2097184 | tf_op jit(solution)/shard_map/all_to_all | solution.py:194
  72.9 2.5 copy.101
  75.4 1.5 copy.102
  76.9 17.9 %reshape.677 = bf16[16,32,32,2,32]{4,3,2,0,1:T(2,128)(2,1)} reshape(bf16[16,16,2,2048]{3,0,2,1:T(8,128)(2,1)} %copy.102) | data formatting | bytes 4194304 | tf_op jit(solution)/shard_map/reshape | solution.py:61
  94.8 12.6 %fusion.20 = bf16[16,32,64,2,64]{4,2,1,0,3:T(8,128)(2,1)} fusion(bf16[16,32,32,2,32,1]{4,3,2,0,1,5:T(2,128)(2,1)} %bitcast.203, bf16[1,32,2,64]{3,1,0,2:T(8,128)(2,1)S(1)} %get-tuple-element.59, bf16[1,32,2,64]{3,1,0,2:T(8,128)(2,1)S(1)} %get-tuple-element.58), kind=kOutput, calls=%fused_computation.24 | convolution fusion | flops 811663360 | bytes 10502144 | tf_op jit(solution)/shard_map/blycz,cydm->blmdz/dot_general | solution.py:65
  107.4 28.7 %fusion.1 = (f32[64,64,64]{2,0,1:T(8,128)}, bf16[16,64,64,2,64]{4,1,2,0,3:T(8,128)(2,1)}) fusion(f32[64,64,64]{2,0,1:T(8,128)} %fusion.29, bf16[16,32,64,2,64]{4,2,1,0,3:T(8,128)(2,1)} %fusion.20, bf16[1,32,2,64]{3,1,0,2:T(8,128)(2,1)S(1)} %get-tuple-element.59, bf16[1,32,2,64]{3,1,0,2:T(8,128)(2,1)S(1)} %get-tuple-element.58), kind=kOutput, calls=%fused_computation.3 | convolution fusion | flops 1107066880 | bytes 27279360 | tf_op jit(solution)/shard_map/bxycz,cxdn->bnydz/dot_general | solution.py:75
  136.1 18.9 %fusion.6 = bf16[16,32,64,2,64,1]{4,1,2,0,3,5:T(8,128)(2,1)} fusion(bf16[16,64,64,2,64]{4,1,2,0,3:T(8,128)(2,1)} %get-tuple-element.42, bf16[1,64,2,32]{1,3,0,2:T(8,128)(2,1)S(1)} %get-tuple-element.57, bf16[1,64,2,32]{1,3,0,2:T(8,128)(2,1)S(1)} %get-tuple-element.56), kind=kOutput, calls=%fused_computation.10 | convolution fusion | flops 1077968896 | bytes 25182208 | tf_op jit(solution)/shard_map/bnydz,dncx->bxycz/dot_general | solution.py:81
  155.0 19.3 %convolution_bitcast_fusion = f32[16,32,32,2,32]{4,2,3,1,0:T(8,128)} fusion(bf16[16,32,64,2,64,1]{4,1,2,0,3,5:T(8,128)(2,1)} %fusion.6, bf16[1,64,2,32]{1,3,0,2:T(8,128)(2,1)S(1)} %get-tuple-element.57, bf16[1,64,2,32]{1,3,0,2:T(8,128)(2,1)S(1)} %get-tuple-element.56), kind=kOutput, calls=%fused_computation.25 | convolution fusion | flops 807469056 | bytes 12599296 | tf_op jit(solution)/shard_map/blydn,dnck->blyck/dot_general | solution.py:94
  174.3 28.6 %copy.138 = f32[16,32,32,2,32]{4,3,2,0,1:T(2,128)} copy(f32[16,32,32,2,32]{4,2,3,1,0:T(8,128)} %convolution_bitcast_fusion) | data formatting | bytes 8388608 | tf_op jit(solution)/shard_map/reshape | solution.py:95
  202.9 21.7 %reshape.699 = f32[16,32,2048]{2,0,1:T(8,128)} reshape(f32[16,32,32,2,32]{4,3,2,0,1:T(2,128)} %copy.138) | data formatting | bytes 8388608 | tf_op jit(solution)/shard_map/reshape | solution.py:95
  224.6 10.1 %all-to-all-start.1 = ((f32[16,32,2048]{2,0,1:T(8,128)}), f32[16,32,2048]{2,0,1:T(8,128)}, u32[]{:S(2)}, u32[]{:S(2)}) async-start(f32[16,32,2048]{2,0,1:T(8,128)} %reshape.699), calls=%async_computation.1 | async-start | bytes 8388608 | tf_op jit(solution)/shard_map/all_to_all | solution.py:200
  234.7 1.3 collective-permute-start
  236.0 3.0 collective-permute-start.1
  239.1 0.1 fusion.83
  239.2 0.1 convert_multiply_fusion.4
  239.3 0.1 convert_multiply_fusion.6
  239.4 5.0 broadcast_multiply_fusion.2
  244.5 3.0 copy.112
  247.5 5.1 reshape.682
  252.7 0.6 multiply_reduce_fusion.3
  254.0 0.6 multiply_reduce_fusion
  256.0 1.8 broadcast_multiply_fusion.4
  257.8 2.5 copy.119
  260.3 3.1 div.129
  263.4 12.6 %fusion.14 = f32[64,768]{1,0:T(8,128)S(1)} fusion(f32[64,4096]{1,0:T(8,128)} %div.129, f32[256,4096]{0,1:T(8,128)} %bitcast.212, f32[256,4096]{0,1:T(8,128)} %bitcast.213, f32[256,4096]{0,1:T(8,128)} %bitcast.211), kind=kOutput, calls=%fused_computation.18 | convolution fusion | flops 2422210560 | bytes 13828096 | tf_op jit(solution)/shard_map/dot_general | solution.py:129
  276.1 0.1 fusion.75
  276.2 36.9 %all-to-all-done.1 = f32[16,32,2048]{2,0,1:T(8,128)} async-done(((f32[16,32,2048]{2,0,1:T(8,128)}), f32[16,32,2048]{2,0,1:T(8,128)}, u32[]{:S(2)}, u32[]{:S(2)}) %all-to-all-start.1) | async-done | bytes 4194336 | tf_op jit(solution)/shard_map/all_to_all | solution.py:200
  313.0 5.5 copy.110
  318.5 4.7 copy.109
  323.2 4.0 copy.143
  327.2 1.9 copy-done.2
  329.1 1.1 fusion.37
  330.2 15.3 %all-reduce = (f32[256]{0:T(256)S(1)}, f32[256]{0:T(256)S(1)}, f32[3,256]{1,0:T(4,128)S(1)}) all-reduce(f32[256]{0:T(256)S(1)} %get-tuple-element.25, f32[256]{0:T(256)S(1)} %get-tuple-element.24, f32[3,256]{1,0:T(4,128)S(1)} %pad_maximum_fusion.9), channel_id=1, replica_groups=mesh['img'=2,'band'=4,'pw'=4] {'pw'}, use_global_device_ids=true, to_apply=%region_5.6 | all-reduce | flops 1280 | bytes 10240 | tf_op jit(solution)/shard_map/psum | solution.py:20
  345.5 19.3 %all-reduce.1 = (f32[256]{0:T(256)S(1)}, f32[256]{0:T(256)S(1)}, f32[3,256]{1,0:T(4,128)S(1)}) all-reduce(f32[256]{0:T(256)S(1)} %get-tuple-element.29, f32[256]{0:T(256)S(1)} %get-tuple-element.30, f32[3,256]{1,0:T(4,128)S(1)} %get-tuple-element.31), channel_id=1, replica_groups=mesh['img'=2,'band'=4,'pw'=4] {'band'}, use_global_device_ids=true, to_apply=%region_6.7 | all-reduce | flops 1280 | bytes 10240 | tf_op jit(solution)/shard_map/psum | solution.py:21
  364.8 0.6 multiply_reduce_fusion.2
  366.1 0.6 broadcast_in_dim.21
  366.7 18.0 %all_to_all.36 = f32[256,2,32,2,32]{4,3,2,0,1:T(2,128)} reshape(f32[16,16,2,2048]{3,1,0,2:T(8,128)} %copy.109) | data formatting | bytes 8388608 | tf_op jit(solution)/shard_map/all_to_all | solution.py:200
  384.6 20.8 %copy.114 = f32[256,2,32,2,32]{0,4,3,2,1:T(8,128)} copy(f32[256,2,32,2,32]{4,3,2,0,1:T(2,128)} %all_to_all.36) | data formatting | bytes 8388608 | tf_op jit(solution)/shard_map/all_to_all | solution.py:200
  405.5 4.6 fusion.41
  410.1 0.8 copy-done.4
  410.9 1.5 divide_convert_fusion
  412.4 0.1 slice_negate_fusion.1
  412.6 0.2 maximum_negate_fusion
  412.8 2.9 copy.115
  415.7 8.2 %multiply_bitcast_fusion = f32[1024,512]{0,1:T(8,128)S(1)} fusion(bf16[1024,4096]{1,0:T(8,128)(2,1)} %bitcast.199, bf16[256,4096]{1,0:T(8,128)(2,1)} %copy.115, bf16[256,4096]{1,0:T(8,128)(2,1)} %fusion.41), kind=kOutput, calls=%fused_computation.59 | convolution fusion | flops 4303880192 | bytes 14680064 | tf_op jit(solution)/shard_map/ik,jk->ij/dot_general | solution.py:218
  423.9 97.3 %all-reduce.3 = bf16[1024,512]{0,1:T(8,128)(2,1)} all-reduce(f32[1024,512]{0,1:T(8,128)S(1)} %multiply_bitcast_fusion), channel_id=1, replica_groups=mesh['img'=2,'band'=4,'pw'=4] {'band','pw'}, use_global_device_ids=true, to_apply=%region_7.8 | all-reduce | flops 524288 | bytes 3145728 | tf_op jit(solution)/shard_map/psum | solution.py:221
  521.3 7.2 %fusion.152 = f32[512,4096]{1,0:T(8,128)S(1)} fusion(bf16[1024,512]{0,1:T(8,128)(2,1)} %all-reduce.3, bf16[1024,4096]{1,0:T(8,128)(2,1)} %bitcast.200), kind=kOutput, calls=%fused_computation.217 | convolution fusion | flops 4294967296 | bytes 17825792 | tf_op jit(solution)/shard_map/ij,ik->jk/dot_general | solution.py:222
  528.5 3.8 fusion.146
  532.2 5.6 copy.116
  537.8 2.8 slice_negate_fusion
  540.6 2.4 pad_maximum_fusion
  543.1 5.4 copy.118
  548.5 6.6 %reshape.680 = f32[1,256,2,2048]{3,2,1,0:T(2,128)} reshape(f32[256,4096]{1,0:T(8,128)} %get-tuple-element.43) | data formatting | bytes 8388608 | tf_op jit(solution)/shard_map/reshape | solution.py:223
  555.0 10.7 %fusion.35 = bf16[1,256,2,2048]{3,1,2,0:T(8,128)(2,1)S(1)} fusion(f32[1,256,2,2048]{3,1,2,0:T(8,128)} %copy.118, f32[1,256,2,2048]{3,2,1,0:T(2,128)} %reshape.680, f32[16,16,2,2048]{3,1,0,2:T(8,128)} %copy.109, f32[1,256,2,2048]{3,2,1,0:T(2,128)} %reshape.682, f32[2,2048]{1,0:T(2,128)S(1)} %get-tuple-element.55, f32[256]{0:T(256)S(1)} %add_divide_fusion, ...), kind=kLoop, calls=%fused_computation.43 | loop fusion | flops 10485760 | bytes 18908160 | tf_op jit(solution)/shard_map/convert_element_type | solution.py:226
  565.7 3.5 copy.120
  (37 shorter events, 0.2 us)
Async XLA Ops:
  0.6 12.1 %copy-start = (bf16[1,1024,256]{2,1,0:T(8,128)(2,1)S(1)}, bf16[1,1024,256]{2,1,0:T(8,128)(2,1)}, u32[]{:S(2)}) copy-start(bf16[1,1024,256]{2,1,0:T(8,128)(2,1)} %param.8) | copy-start | bytes 1572868
  18.5 11.8 %copy-start.9 = (s32[256]{0:T(256)S(1)}, s32[256]{0:T(256)}, u32[]{:S(2)}) copy-start(s32[256]{0:T(256)} %param.12) | copy-start | bytes 3076
  18.5 11.8 %copy-start.10 = (f32[4]{0:T(128)S(1)}, f32[4]{0:T(128)}, u32[]{:S(2)}) copy-start(f32[4]{0:T(128)} %param.13) | copy-start | bytes 52
  18.5 11.9 %copy-start.5 = (s32[1,3,256]{2,0,1:T(1,128)S(1)}, s32[1,3,256]{2,0,1:T(1,128)}, u32[]{:S(2)}) copy-start(s32[1,3,256]{2,0,1:T(1,128)} %param.9) | copy-start | bytes 9220
  21.3 51.6 %all-to-all-start = ((bf16[256,2,2048]{2,1,0:T(2,128)(2,1)}), bf16[256,2,2048]{2,1,0:T(2,128)(2,1)}, u32[]{:S(2)}, u32[]{:S(2)}) async-start(bf16[256,2,2048]{2,1,0:T(2,128)(2,1)} %reshape.676), calls=%async_computation | async-start | bytes 4194304 | tf_op jit(solution)/shard_map/all_to_all | solution.py:194
  224.6 88.5 %all-to-all-start.1 = ((f32[16,32,2048]{2,0,1:T(8,128)}), f32[16,32,2048]{2,0,1:T(8,128)}, u32[]{:S(2)}, u32[]{:S(2)}) async-start(f32[16,32,2048]{2,0,1:T(8,128)} %reshape.699), calls=%async_computation.1 | async-start | bytes 8388608 | tf_op jit(solution)/shard_map/all_to_all | solution.py:200
  234.7 18.0 %collective-permute-start = (s32[3,256]{1,0:T(4,128)S(1)}, s32[3,256]{1,0:T(4,128)S(1)}, u32[]{:S(2)}, u32[]{:S(2)}) collective-permute-start(s32[3,256]{1,0:T(4,128)S(1)} %bitcast.224), channel_id=1, source_target_pairs={{16,0},{17,1},{18,2},{19,3},{20,4},{21,5},{22,6},{23,7},{24,8},{25... | collective-permute-start | bytes 9224 | tf_op jit(solution)/shard_map/ppermute | solution.py:27
  236.0 16.7 %collective-permute-start.1 = (s32[3,256]{1,0:T(4,128)S(1)}, s32[3,256]{1,0:T(4,128)S(1)}, u32[]{:S(2)}, u32[]{:S(2)}) collective-permute-start(s32[3,256]{1,0:T(4,128)S(1)} %bitcast.225), channel_id=1, source_target_pairs={{0,16},{1,17},{2,18},{3,19},{4,20},{5,21},{6,22},{7,23},{8,24},{9,... | collective-permute-start | bytes 9224 | tf_op jit(solution)/shard_map/ppermute | solution.py:27
  247.5 5.2 copy-start.7
  247.5 5.2 copy-start.8
  327.2 1.9 copy-start.2
  405.5 149.6 %copy-start.6 = (f32[256]{0:T(256)}, f32[256]{0:T(256)S(1)}, u32[]{:S(2)}) copy-start(f32[256]{0:T(256)S(1)} %add_divide_fusion) | copy-start | bytes 3076
  405.5 4.7 copy-start.3
  405.5 5.5 copy-start.4
  555.0 14.2 %copy-start.1 = (bf16[1,1024,256]{2,1,0:T(8,128)(2,1)S(1)}, bf16[1,1024,256]{2,1,0:T(8,128)(2,1)}, u32[]{:S(2)}) copy-start(bf16[1,1024,256]{2,1,0:T(8,128)(2,1)} %param.8) | copy-start | bytes 1572868
